TPU v7x, 512 devices: a whole 4x8x8 slice. The times are simulated.
512 devices in a mesh: seq: 64 (over y, x, z_hi), tp: 8 (over z_lo, core).
Axes of the slice: x: 4, y: 8, z: 8 (z_hi: 2, z_lo: 4; z = z_hi * 4 + z_lo), core: 2. Of those that a mesh axis runs over, the one named last changes fastest.
Arguments:
- queries: bfloat16 [16384, 4096], P('seq', 'tp'), may hold values from -90 to 90
- key_rows: bfloat16 [16384, 4096], P('seq', 'tp'), may hold values from -4 to 4
- value_rows: bfloat16 [16384, 4096], P('seq', 'tp'), may hold values from -5 to 5
- residual: bfloat16 [16384, 4096], P('seq', 'tp'), may hold values from -1.5 to 1.5
- out_weight: bfloat16 [4096, 4096], P('tp', 'seq'), may hold values from -0.09375 to 0.09375
- norm_gain: float32 [4096], P('tp'), may hold values from 0.5 to 1.5
- norm_bias: float32 [4096], P('tp'), may hold values from -1 to 1
- global_list: int32 [2], replicated, may hold values from 0 to 1023
- random_device: int32 [1024, 3], P('seq'), may hold values from 0 to 63, all different within a row; in each aligned block of 16 rows (0 to 15, 16 to 31, ...) at most 2 rows name the same one
- random_offset: int32 [1024, 3], P('seq'), may hold values from 0 to 15
- drop_seed: int32 [1], replicated, may hold values from 0 to 65535
- drop_offsets: int32 [1024], P('seq'), may hold values from 0 to 8388607
Outputs:
- encoded: bfloat16 [16384, 4096], P('seq', 'tp')
Inputs may be any that keep to these rules, and one draw needn't show every extreme that they name: `random_device`: each row names 3 different indices; among the 16 rows of one index of seq no index is named more than 2 times.
All inputs are finite; a program needn't handle non-finite values.
Results may differ from a plain program's by a relative error of at most 0.013.
Values may be sent and summed in bfloat16 or wider, within the bound.
No kernel may reach another device: no remote copies, remote signals or barrier semaphores. Data moves between devices by JAX's collectives and lax.ppermute only.
A program may use at most 64 MiB of HBM per device.

v0:
```python
import jax
import jax.numpy as jnp
from jax import lax
from jax.sharding import PartitionSpec as P

D = 4096
DH = 128
BLOCK = 16


def padded_2(x, sides, width):
    for axis, dim in sides:
        devices, length = (lax.axis_size(axis), x.shape[dim])
        up = [(i, (i + 1) % devices) for i in range(devices)]
        down = [(j, i) for i, j in up]
        last = lax.slice_in_dim(x, length - width, length, axis=dim)
        first = lax.slice_in_dim(x, 0, width, axis=dim)
        before = lax.ppermute(last, axis, up)
        after = lax.ppermute(first, axis, down)
        x = jnp.concatenate([before, x, after], axis=dim)
    return x


def broadcast(value, axis, source):
    kept = jnp.where(lax.axis_index(axis) == source, value, 0).astype(value.dtype)
    return lax.psum(kept, axis)


def mix_bits(counter, seed_value):
    hashed = counter + seed_value * 1000003
    for rounds in range(2):
        hashed = jnp.bitwise_xor(hashed, lax.shift_right_logical(hashed, jnp.int32(16)))
        hashed = hashed * 73244475
    hashed = jnp.bitwise_xor(hashed, lax.shift_right_logical(hashed, jnp.int32(16)))
    return hashed


def keep_table(counter, seed_value):
    hashed = mix_bits(counter, seed_value)
    kept = jnp.bitwise_and(hashed, 1023) >= 102
    return jnp.where(kept, jnp.float32(1024.0 / 922.0), jnp.float32(0.0))


def on_device(
    queries,
    key_rows,
    value_rows,
    residual,
    out_weight,
    norm_gain,
    norm_bias,
    global_list,
    random_device,
    random_offset,
    drop_seed,
    drop_offsets,
):
    row_count, width_here = queries.shape
    heads_here = width_here // DH
    block_count = row_count // BLOCK
    seq_count = lax.axis_size("seq")
    paired = jnp.concatenate([key_rows, value_rows], axis=1).reshape(
        block_count, BLOCK, 2 * width_here
    )
    padded = padded_2(paired, (("seq", 0),), 1)
    window = jnp.stack(
        [padded[0:block_count], padded[1 : block_count + 1], padded[2 : block_count + 2]], axis=1
    )
    glob_count = global_list.shape[0]
    fetched = []
    for which in range(glob_count):
        wanted_block = global_list[which]
        local_block = jnp.take(paired, wanted_block % block_count, axis=0)
        fetched.append(broadcast(local_block, "seq", wanted_block // block_count))
    glob_blocks = jnp.stack(fetched, axis=0)
    glob_blocks = jnp.broadcast_to(glob_blocks[None], (block_count,) + glob_blocks.shape)
    rand_count = random_device.shape[1]
    request_count = block_count * rand_count
    target = random_device.reshape(request_count)
    wanted = random_offset.reshape(request_count)
    request_rank = jnp.arange(request_count, dtype=jnp.int32)
    same_dest = target[:, None] == target[None, :]
    earlier = request_rank[None, :] < request_rank[:, None]
    slot_index = jnp.sum(jnp.logical_and(same_dest, earlier), axis=1)
    capacity = max(2, -(-request_count // seq_count))
    dest_ids = jnp.arange(seq_count, dtype=jnp.int32)
    slot_ids = jnp.arange(capacity, dtype=jnp.int32)
    matched = jnp.logical_and(
        target[None, None, :] == dest_ids[:, None, None],
        slot_index[None, None, :] == slot_ids[None, :, None],
    )
    request_table = jnp.sum(jnp.where(matched, wanted[None, None, :], 0), axis=2)
    picked = jnp.take(
        paired,
        lax.all_to_all(request_table, "seq", split_axis=0, concat_axis=0, tiled=True),
        axis=0,
    )
    replies = lax.all_to_all(picked, "seq", split_axis=0, concat_axis=0, tiled=True)
    flat_replies = replies.reshape(seq_count * capacity, BLOCK, 2 * width_here)
    chosen = jnp.take(flat_replies, target * capacity + slot_index, axis=0)
    chosen = chosen.reshape(block_count, rand_count, BLOCK, 2 * width_here)
    all_keys = jnp.concatenate([window, glob_blocks, chosen], axis=1)
    key_total = all_keys.shape[1] * BLOCK
    all_keys = all_keys.reshape(block_count, key_total, 2 * width_here)
    key_heads = all_keys[:, :, :width_here].reshape(block_count, key_total, heads_here, DH)
    value_heads = all_keys[:, :, width_here:].reshape(block_count, key_total, heads_here, DH)
    query_heads = queries.reshape(block_count, BLOCK, heads_here, DH)
    score_scale = jnp.float32(1.0 / DH**0.5)
    scores = (
        jnp.einsum("bqhd,bkhd->bhqk", query_heads, key_heads, preferred_element_type=jnp.float32)
        * score_scale
    )
    top_score = jnp.max(scores, axis=-1, keepdims=True)
    expo = jnp.exp(scores - top_score)
    attn_probs = (expo / jnp.sum(expo, axis=-1, keepdims=True)).astype(jnp.bfloat16)
    context = jnp.einsum(
        "bhqk,bkhd->bqhd", attn_probs, value_heads, preferred_element_type=jnp.float32
    )
    context = context.astype(jnp.bfloat16).reshape(row_count, width_here)
    partial_terms = jnp.dot(
        context,
        lax.all_gather(out_weight, "seq", axis=1, tiled=True),
        preferred_element_type=jnp.float32,
    )
    attended = lax.psum_scatter(
        partial_terms.astype(jnp.bfloat16), "tp", scatter_dimension=1, tiled=True
    ).astype(jnp.float32)
    cols_here = attended.shape[1]
    first_col = lax.axis_index("tp") * cols_here
    inner = jnp.arange(BLOCK, dtype=jnp.int32)
    columns = first_col + jnp.arange(cols_here, dtype=jnp.int32)
    counter = drop_offsets[:, None, None] + inner[None, :, None] * D + columns[None, None, :]
    keep_factor = keep_table(counter, drop_seed[0]).reshape(row_count, cols_here)
    summed_rows = residual.astype(jnp.float32) + keep_factor * attended
    row_total = lax.psum(jnp.sum(summed_rows, axis=1), "tp")
    row_mean = row_total / D
    centered = summed_rows - row_mean[:, None]
    spread = lax.psum(jnp.sum(centered * centered, axis=1), "tp")
    row_var = spread / D
    encoded = (
        centered * lax.rsqrt(row_var + 1e-05)[:, None] * norm_gain[None, :] + norm_bias[None, :]
    )
    return encoded.astype(jnp.bfloat16)


def solution(mesh):
    placed = (
        P("seq", "tp"),
        P("seq", "tp"),
        P("seq", "tp"),
        P("seq", "tp"),
        P("tp", "seq"),
        P("tp"),
        P("tp"),
        P(),
        P("seq", None),
        P("seq", None),
        P(),
        P("seq"),
    )
    return jax.shard_map(
        on_device, mesh=mesh, in_specs=placed, out_specs=P("seq", "tp"), check_vma=False
    )
```

profile of v0, /device:TPU:1, one launch (start us, length us, event | category | flops | bytes accessed | tf_op | source)
XLA Modules:
  0.0 1136.7 jit_solution(4310646254590320187)
XLA Ops:
  9.3 19.6 %all-to-all-start = ((s32[64,1,2]{2,1,0:T(1,128)}), s32[64,1,2]{2,1,0:T(1,128)S(1)}, u32[]{:S(2)}, u32[]{:S(2)}) async-start(s32[64,1,2]{2,1,0:T(1,128)} %copy.71), calls=%async_computation | async-start | bytes 65536 | tf_op jit(solution)/shard_map/all_to_all | solution.py:95
  28.9 1.0 constant_dynamic-update-slice_fusion.1
  29.9 1.0 constant_dynamic-update-slice_fusion
  30.9 11.2 all-to-all-done
  42.5 2.7 gather_fusion
  45.2 4.6 broadcast_select_fusion
  49.9 5.8 all-to-all-start.1
  63.3 6.6 collective-permute-start
  69.9 6.8 collective-permute-start.1
  77.0 73.8 %collective-permute-done = bf16[1,16,1024]{2,1,0:T(8,128)(2,1)S(1)} collective-permute-done((bf16[1,16,1024]{2,1,0:T(8,128)(2,1)S(1)}, bf16[1,16,1024]{2,1,0:T(8,128)(2,1)S(1)}, u32[]{:S(2)}, u32[]{:S(2)}) %collective-permute-start) | collective-permute-done | bytes 32800 | tf_op jit(solution)/shard_map/ppermute | solution.py:18
  153.4 702.0 %all-reduce.3.cloned.1.call-done = (bf16[1,16,1024]{2,1,0:T(8,128)(2,1)}, bf16[1,16,1024]{2,1,0:T(8,128)(2,1)}) async-done(((bf16[1,16,1024]{2,1,0:T(8,128)(2,1)}, bf16[1,16,1024]{2,1,0:T(8,128)(2,1)}), (bf16[1,16,1024]{2,1,0:T(8,128)(2,1)}, bf16[1,16,1024]{2,1,0:T(8,128)(2,1)})) %all-reduce.3.cloned.1.call-update) | async-done | bytes 65552 | tf_op jit(solution)/shard_map/psum | solution.py:26
  856.2 1.1 broadcast_dynamic-update-slice_fusion
  857.3 2.8 gather_fusion.1
  860.1 1.5 select_dynamic-update-slice_fusion
  861.6 4.6 fusion.23
  866.3 3.0 copy.80
  869.3 3.9 copy.79
  874.3 3.4 fusion.4
  877.8 175.0 %all-gather.2.cloned.1.call-done = bf16[512,4096]{0,1:T(8,128)(2,1)} async-done(((bf16[512,64]{0,1:T(8,128)(2,1)}), bf16[512,4096]{0,1:T(8,128)(2,1)}) %all-gather.2.cloned.1.call-update) | async-done | bytes 4194320 | tf_op jit(solution)/shard_map/all_gather | solution.py:122
  1052.8 4.8 convolution_convert_fusion
  1058.6 38.0 %reduce-scatter.2.cloned.1.call-done = bf16[256,512]{1,0:T(8,128)(2,1)} async-done(((bf16[256,4096]{1,0:T(8,128)(2,1)}), bf16[256,512]{1,0:T(8,128)(2,1)}) %reduce-scatter.2.cloned.1.call-update) | async-done | bytes 262160 | tf_op jit(solution)/shard_map/reduce_scatter | solution.py:125
  1096.6 1.4 fusion.22
  1098.1 16.2 %psum.30 = f32[256]{0:T(256)S(1)} all-reduce(f32[256]{0:T(256)S(1)} %get-tuple-element.19), channel_id=1, replica_groups=mesh['seq'=64,'tp'=8] {'tp'}, use_global_device_ids=true, to_apply=%region_8.10 | all-reduce | flops 256 | bytes 2048 | tf_op jit(solution)/shard_map/psum | solution.py:135
  1114.5 14.8 %psum.31 = f32[256]{0:T(256)S(1)} all-reduce(f32[256]{0:T(256)S(1)} %multiply_reduce_fusion), channel_id=1, replica_groups=mesh['seq'=64,'tp'=8] {'tp'}, use_global_device_ids=true, to_apply=%region_10.12 | all-reduce | flops 256 | bytes 2048 | tf_op jit(solution)/shard_map/psum | solution.py:138
  (64 shorter events, 11.5 us)
Async XLA Ops:
  9.3 32.7 %all-to-all-start = ((s32[64,1,2]{2,1,0:T(1,128)}), s32[64,1,2]{2,1,0:T(1,128)S(1)}, u32[]{:S(2)}, u32[]{:S(2)}) async-start(s32[64,1,2]{2,1,0:T(1,128)} %copy.71), calls=%async_computation | async-start | bytes 65536 | tf_op jit(solution)/shard_map/all_to_all | solution.py:95
  49.9 5.9 copy-start.4
  49.9 27.1 %copy-start = (bf16[256,512]{1,0:T(8,128)(2,1)S(1)}, bf16[256,512]{1,0:T(8,128)(2,1)}, u32[]{:S(2)}) copy-start(bf16[256,512]{1,0:T(8,128)(2,1)} %param.14) | copy-start | bytes 786436
  49.9 807.4 %all-to-all-start.1 = ((bf16[64,2,16,1024]{3,2,1,0:T(8,128)(2,1)}), bf16[64,2,16,1024]{3,2,1,0:T(8,128)(2,1)}, u32[]{:S(2)}, u32[]{:S(2)}) async-start(bf16[64,2,16,1024]{3,2,1,0:T(8,128)(2,1)} %broadcast_select_fusion), calls=%async_computation.1 | async-start | bytes 8388608 | tf_op jit(solution)/shard_map/all_to_all | solution.py:98
  55.7 799.7 %all-reduce.3.cloned.1.call-start = ((), (), s32[]{:S(2)}) async-start(), calls=%async_computation.5 | async-start | bytes 131072 | tf_op jit(solution)/shard_map/psum | solution.py:26
  62.5 990.3 %all-gather.2.cloned.1.call-start = ((), (), s32[]{:S(2)}) async-start(), calls=%async_computation.3 | async-start | bytes 4259840 | tf_op jit(solution)/shard_map/all_gather | solution.py:122
  63.2 1033.4 %reduce-scatter.2.cloned.1.call-start = ((), (), s32[]{:S(2)}) async-start(), calls=%async_computation.4 | async-start | bytes 2359296 | tf_op jit(solution)/shard_map/reduce_scatter | solution.py:125
  63.3 87.6 %collective-permute-start = (bf16[1,16,1024]{2,1,0:T(8,128)(2,1)S(1)}, bf16[1,16,1024]{2,1,0:T(8,128)(2,1)S(1)}, u32[]{:S(2)}, u32[]{:S(2)}) collective-permute-start(bf16[1,16,1024]{2,1,0:T(8,128)(2,1)S(1)} %get-tuple-element.26), channel_id=1, source_target_pairs={{0,8},{8,16},{16,24},{24,32},{32,40},{40,48},{48,56},{56,64},{64,7... | collective-permute-start | bytes 98312 | tf_op jit(solution)/shard_map/ppermute | solution.py:18
  69.9 82.6 %collective-permute-start.1 = (bf16[1,16,1024]{2,1,0:T(8,128)(2,1)S(1)}, bf16[1,16,1024]{2,1,0:T(8,128)(2,1)S(1)}, u32[]{:S(2)}, u32[]{:S(2)}) collective-permute-start(bf16[1,16,1024]{2,1,0:T(8,128)(2,1)S(1)} %get-tuple-element.25), channel_id=1, source_target_pairs={{8,0},{16,8},{24,16},{32,24},{40,32},{48,40},{56,48},{64,56},{72,6... | collective-permute-start | bytes 98312 | tf_op jit(solution)/shard_map/ppermute | solution.py:19
  1052.8 5.0 copy-start.5
  1052.8 43.9 %copy-start.1 = (bf16[256,512]{1,0:T(8,128)(2,1)S(1)}, bf16[256,512]{1,0:T(8,128)(2,1)}, u32[]{:S(2)}) copy-start(bf16[256,512]{1,0:T(8,128)(2,1)} %param.17) | copy-start | bytes 786436
  1052.8 76.6 %copy-start.2 = (f32[512]{0:T(512)S(1)}, f32[512]{0:T(512)}, u32[]{:S(2)}) copy-start(f32[512]{0:T(512)} %param.20) | copy-start | bytes 6148
  1052.8 76.6 %copy-start.3 = (f32[512]{0:T(512)S(1)}, f32[512]{0:T(512)}, u32[]{:S(2)}) copy-start(f32[512]{0:T(512)} %param.19) | copy-start | bytes 6148
Sparse Core Ops, SparseCore 0:
  62.6 792.7 all-reduce.2
  860.7 191.9 all-gather.1
  1057.8 38.8 reduce-scatter.1
where the time goes:
time: 1140 us
  waiting for transfers between devices  1000 us (88%)
  starting transfers between devices  38.9 us (3%)
  blocking collectives  31.1 us (3%)
  local copies, waits for them, and re-layouts  25.2 us (2%)
  between operations  19.4 us (2%)
  other arithmetic  12.5 us (1%)
    psum x1, waiting for transfers between devices, broadcast(): return lax.psum(kept, axis)  702 us
    all_gather x1, waiting for transfers between devices, on_device(): lax.all_gather(out_weight, 'seq', axis=1, tiled=True)  175 us
    ppermute x1, waiting for transfers between devices, padded_2(): before = lax.ppermute(last, axis, up)  73.8 us
    reduce_scatter x1, waiting for transfers between devices, on_device(): lax.psum_scatter(partial_terms.astype(jnp.bfloat16), 'tp', scatter_dimens...  38 us
  transfers between devices with their start and end apart: 7, of which 5 were waited for; matrix products, arithmetic and copies ran while one was open for 3% of the time, Pallas kernels for 0%

commit v1 on v0

--- a/solution.py
+++ b/solution.py
@@ -23,7 +23,12 @@
 
 def broadcast(value, axis, source):
     kept = jnp.where(lax.axis_index(axis) == source, value, 0).astype(value.dtype)
-    return lax.psum(kept, axis)
+
+    def _name_series_all(in_array):
+        mid_arr = jnp.sum(lax.all_gather(in_array, axis), axis=0)
+        return mid_arr
+
+    return _name_series_all(kept)
 
 
 def mix_bits(counter, seed_value):

time: 1140 us -> 613 us (0.54)
  waiting for transfers between devices: 1000 us -> 460 us
  blocking collectives: 31.1 us -> 63.6 us
  starting transfers between devices: 38.9 us -> 19.3 us
    psum x1 -> x0, waiting for transfers between devices: 702 us -> none  [broadcast(): return lax.psum(kept, axis)]
    all_gather x0 -> x2, waiting for transfers between devices: none -> 207 us  [_name_series_all(): mid_arr = jnp.sum(lax.all_gather(in_array, axis), axis=0)]
    all_gather x1, waiting for transfers between devices: 175 us -> 133 us  [on_device(): lax.all_gather(out_weight, 'seq', axis=1, tiled=True)]
    all_to_all x0 -> x1, blocking collectives: none -> 32.6 us  [on_device(): lax.all_to_all(request_table, 'seq', split_axis=0, concat_axis=0, tiled=T...]
    all_to_all x1 -> x0, starting transfers between devices: 19.6 us -> none  [on_device(): lax.all_to_all(request_table, 'seq', split_axis=0, concat_axis=0, tiled=T...]
  transfers between devices with their start and end apart: 7 -> 7, of which waited for: 5 -> 5; matrix products, arithmetic and copies ran while one was open for 3% -> 6% of each run, Pallas kernels for 0% -> 0%
where the time goes in v1:
time: 613 us; the launch traced here: 612 us
  waiting for transfers between devices  460 us (75%)
  blocking collectives  63.6 us (10%)
  local copies, waits for them, and re-layouts  25.4 us (4%)
  between operations  19.4 us (3%)
  starting transfers between devices  19.3 us (3%)
  other arithmetic  15.6 us (3%)
  matrix products  8.9 us (1%)
    all_gather x2, waiting for transfers between devices, _name_series_all(): mid_arr = jnp.sum(lax.all_gather(in_array, axis), axis=0)  207 us
    all_gather x1, waiting for transfers between devices, on_device(): lax.all_gather(out_weight, 'seq', axis=1, tiled=True)  133 us
    ppermute x1, waiting for transfers between devices, padded_2(): before = lax.ppermute(last, axis, up)  80.9 us
    reduce_scatter x1, waiting for transfers between devices, on_device(): lax.psum_scatter(partial_terms.astype(jnp.bfloat16), 'tp', scatter_dimens...  38 us
    all_to_all x1, blocking collectives, on_device(): lax.all_to_all(request_table, 'seq', split_axis=0, concat_axis=0, tiled=T...  32.6 us
    psum x1, blocking collectives, on_device(): row_total = lax.psum(jnp.sum(summed_rows, axis=1), 'tp')  16.2 us
    psum x1, blocking collectives, on_device(): spread = lax.psum(jnp.sum(centered * centered, axis=1), 'tp')  14.9 us
  transfers between devices with their start and end apart: 7, of which 5 were waited for; matrix products, arithmetic and copies ran while one was open for 6% of the time, Pallas kernels for 0%

profile of v1, /device:TPU:1, one launch (start us, length us, event | category | flops | bytes accessed | tf_op | source)
XLA Modules:
  0.0 612.5 jit_solution(10002710435305056970)
XLA Ops:
  6.5 1.4 fusion.22
  18.9 32.6 %all_to_all.20 = s32[64,1,2]{2,1,0:T(1,128)S(1)} all-to-all(s32[64,1,2]{2,1,0:T(1,128)S(1)} %copy.70), channel_id=1, replica_groups=mesh['seq'=64,'tp'=8] {'seq'}, dimensions={0} | all-to-all | bytes 1024 | tf_op jit(solution)/shard_map/all_to_all | solution.py:100
  51.8 2.7 gather_fusion
  54.7 4.6 broadcast_select_fusion
  59.3 5.8 all-to-all-start.1
  65.9 6.6 %collective-permute-start = (bf16[1,16,1024]{2,1,0:T(8,128)(2,1)S(1)}, bf16[1,16,1024]{2,1,0:T(8,128)(2,1)S(1)}, u32[]{:S(2)}, u32[]{:S(2)}) collective-permute-start(bf16[1,16,1024]{2,1,0:T(8,128)(2,1)S(1)} %get-tuple-element.24), channel_id=1, source_target_pairs={{0,8},{8,16},{16,24},{24,32},{32,40},{40,48},{48,56},{56,64},{64,7... | collective-permute-start | bytes 98312 | tf_op jit(solution)/shard_map/ppermute | solution.py:18
  72.6 6.8 %collective-permute-start.1 = (bf16[1,16,1024]{2,1,0:T(8,128)(2,1)S(1)}, bf16[1,16,1024]{2,1,0:T(8,128)(2,1)S(1)}, u32[]{:S(2)}, u32[]{:S(2)}) collective-permute-start(bf16[1,16,1024]{2,1,0:T(8,128)(2,1)S(1)} %get-tuple-element.23), channel_id=1, source_target_pairs={{8,0},{16,8},{24,16},{32,24},{40,32},{48,40},{56,48},{64,56},{72,6... | collective-permute-start | bytes 98312 | tf_op jit(solution)/shard_map/ppermute | solution.py:19
  79.7 80.9 %collective-permute-done = bf16[1,16,1024]{2,1,0:T(8,128)(2,1)S(1)} collective-permute-done((bf16[1,16,1024]{2,1,0:T(8,128)(2,1)S(1)}, bf16[1,16,1024]{2,1,0:T(8,128)(2,1)S(1)}, u32[]{:S(2)}, u32[]{:S(2)}) %collective-permute-start) | collective-permute-done | bytes 32800 | tf_op jit(solution)/shard_map/ppermute | solution.py:18
  163.1 72.1 %all-gather.8.cloned.1.call-done = bf16[1024,1024]{1,0:T(8,128)(2,1)} async-done(((bf16[16,1024]{1,0:T(8,128)(2,1)}), bf16[1024,1024]{1,0:T(8,128)(2,1)}) %all-gather.8.cloned.1.call-update) | async-done | bytes 2097168 | tf_op jit(solution)/shard_map/all_gather | solution.py:28
  235.2 1.9 reduce_sum.73
  237.1 134.9 %all-gather.10.cloned.1.call-done = bf16[1024,1024]{1,0:T(8,128)(2,1)} async-done(((bf16[16,1024]{1,0:T(8,128)(2,1)}), bf16[1024,1024]{1,0:T(8,128)(2,1)}) %all-gather.10.cloned.1.call-update) | async-done | bytes 2097168 | tf_op jit(solution)/shard_map/all_gather | solution.py:28
  372.0 1.9 reduce_sum.74
  375.1 2.8 gather_fusion.1
  378.0 1.5 select_dynamic-update-slice_fusion
  379.4 4.6 fusion.21
  384.1 3.0 copy.79
  387.1 3.9 copy.78
  392.1 3.4 fusion.4
  395.6 132.9 %all-gather.6.cloned.1.call-done = bf16[512,4096]{0,1:T(8,128)(2,1)} async-done(((bf16[512,64]{0,1:T(8,128)(2,1)}), bf16[512,4096]{0,1:T(8,128)(2,1)}) %all-gather.6.cloned.1.call-update) | async-done | bytes 4194320 | tf_op jit(solution)/shard_map/all_gather | solution.py:127
  528.6 4.9 convolution_convert_fusion
  534.4 38.0 %reduce-scatter.2.cloned.1.call-done = bf16[256,512]{1,0:T(8,128)(2,1)} async-done(((bf16[256,4096]{1,0:T(8,128)(2,1)}), bf16[256,512]{1,0:T(8,128)(2,1)}) %reduce-scatter.2.cloned.1.call-update) | async-done | bytes 262160 | tf_op jit(solution)/shard_map/reduce_scatter | solution.py:130
  572.4 1.4 fusion.20
  573.8 16.2 %psum.14 = f32[256]{0:T(256)S(1)} all-reduce(f32[256]{0:T(256)S(1)} %get-tuple-element.17), channel_id=1, replica_groups=mesh['seq'=64,'tp'=8] {'tp'}, use_global_device_ids=true, to_apply=%region_8.10 | all-reduce | flops 256 | bytes 2048 | tf_op jit(solution)/shard_map/psum | solution.py:140
  590.2 14.9 %psum.15 = f32[256]{0:T(256)S(1)} all-reduce(f32[256]{0:T(256)S(1)} %multiply_reduce_fusion), channel_id=1, replica_groups=mesh['seq'=64,'tp'=8] {'tp'}, use_global_device_ids=true, to_apply=%region_10.12 | all-reduce | flops 256 | bytes 2048 | tf_op jit(solution)/shard_map/psum | solution.py:143
  (66 shorter events, 13.2 us)
Async XLA Ops:
  6.5 228.6 %all-gather.8.cloned.1.call-start = ((), (), s32[]{:S(2)}) async-start(), calls=%async_computation.5 | async-start | bytes 2129920 | tf_op jit(solution)/shard_map/all_gather | solution.py:28
  16.0 356.1 %all-gather.10.cloned.1.call-start = ((), (), s32[]{:S(2)}) async-start(), calls=%async_computation.6 | async-start | bytes 2129920 | tf_op jit(solution)/shard_map/all_gather | solution.py:28
  59.3 20.3 %copy-start = (bf16[256,512]{1,0:T(8,128)(2,1)S(1)}, bf16[256,512]{1,0:T(8,128)(2,1)}, u32[]{:S(2)}) copy-start(bf16[256,512]{1,0:T(8,128)(2,1)} %param.14) | copy-start | bytes 786436
  59.3 315.8 %all-to-all-start.1 = ((bf16[64,2,16,1024]{3,2,1,0:T(8,128)(2,1)}), bf16[64,2,16,1024]{3,2,1,0:T(8,128)(2,1)}, u32[]{:S(2)}, u32[]{:S(2)}) async-start(bf16[64,2,16,1024]{3,2,1,0:T(8,128)(2,1)} %broadcast_select_fusion), calls=%async_computation.1 | async-start | bytes 8388608 | tf_op jit(solution)/shard_map/all_to_all | solution.py:103
  65.1 463.4 %all-gather.6.cloned.1.call-start = ((), (), s32[]{:S(2)}) async-start(), calls=%async_computation.3 | async-start | bytes 4259840 | tf_op jit(solution)/shard_map/all_gather | solution.py:127
  65.9 506.6 %reduce-scatter.2.cloned.1.call-start = ((), (), s32[]{:S(2)}) async-start(), calls=%async_computation.4 | async-start | bytes 2359296 | tf_op jit(solution)/shard_map/reduce_scatter | solution.py:130
  65.9 94.7 %collective-permute-start = (bf16[1,16,1024]{2,1,0:T(8,128)(2,1)S(1)}, bf16[1,16,1024]{2,1,0:T(8,128)(2,1)S(1)}, u32[]{:S(2)}, u32[]{:S(2)}) collective-permute-start(bf16[1,16,1024]{2,1,0:T(8,128)(2,1)S(1)} %get-tuple-element.24), channel_id=1, source_target_pairs={{0,8},{8,16},{16,24},{24,32},{32,40},{40,48},{48,56},{56,64},{64,7... | collective-permute-start | bytes 98312 | tf_op jit(solution)/shard_map/ppermute | solution.py:18
  72.6 89.7 %collective-permute-start.1 = (bf16[1,16,1024]{2,1,0:T(8,128)(2,1)S(1)}, bf16[1,16,1024]{2,1,0:T(8,128)(2,1)S(1)}, u32[]{:S(2)}, u32[]{:S(2)}) collective-permute-start(bf16[1,16,1024]{2,1,0:T(8,128)(2,1)S(1)} %get-tuple-element.23), channel_id=1, source_target_pairs={{8,0},{16,8},{24,16},{32,24},{40,32},{48,40},{56,48},{64,56},{72,6... | collective-permute-start | bytes 98312 | tf_op jit(solution)/shard_map/ppermute | solution.py:19
  528.5 5.0 copy-start.4
  528.6 43.9 %copy-start.1 = (bf16[256,512]{1,0:T(8,128)(2,1)S(1)}, bf16[256,512]{1,0:T(8,128)(2,1)}, u32[]{:S(2)}) copy-start(bf16[256,512]{1,0:T(8,128)(2,1)} %param.17) | copy-start | bytes 786436
  528.6 76.5 %copy-start.2 = (f32[512]{0:T(512)S(1)}, f32[512]{0:T(512)}, u32[]{:S(2)}) copy-start(f32[512]{0:T(512)} %param.20) | copy-start | bytes 6148
  528.6 76.5 %copy-start.3 = (f32[512]{0:T(512)S(1)}, f32[512]{0:T(512)}, u32[]{:S(2)}) copy-start(f32[512]{0:T(512)} %param.19) | copy-start | bytes 6148
Sparse Core Ops, SparseCore 0:
  16.1 219.0 all-gather.7
  239.7 132.3 all-gather.9
  376.6 151.9 all-gather.5
  533.6 38.8 reduce-scatter.1
